TPU v7x, 128 devices: a whole 4x4x4 slice. The times are simulated.
128 devices in a mesh: replica: 16 (over x_lo, z, core), tensor: 8 (over y, x_hi).
Axes of the slice: x: 4 (x_hi: 2, x_lo: 2; x = x_hi * 2 + x_lo), y: 4, z: 4, core: 2. Of those that a mesh axis runs over, the one named last changes fastest.
Arguments:
- tokens: bfloat16 [8192, 1024], P('replica'), may hold values from -6 to 6
- targets: bfloat16 [8192, 1024], P('replica'), may hold values from -6 to 6
- row_ids: int32 [16, 3, 512], P('replica'), may hold values from 0 to 511
- anchor: float32 [2, 1024, 4096], P(None, None, 'tensor'), may hold values from -0.1875 to 0.1875
- momentum: float32 [16, 2, 1024, 4096], P('replica', None, None, 'tensor'), may hold values from -4 to 4
- slow: float32 [2, 1024, 4096], P(None, None, 'tensor'), may hold values from -6 to 6
Outputs:
- anchor_new: float32 [2, 1024, 4096], P(None, None, 'tensor')
- slow_new: float32 [2, 1024, 4096], P(None, None, 'tensor')
- momentum_new: float32 [16, 2, 1024, 4096], P('replica', None, None, 'tensor')
Inputs may be any that keep to these rules, and one draw needn't show every extreme that they name: `row_ids`: each id names a row within its replica's own block of 512 rows; rows may repeat.
All inputs are finite; a program needn't handle non-finite values.
Results may differ from a plain program's by a relative error of at most 0.008.
Values may be sent and summed in bfloat16 or wider, within the bound.
A program may use at most 128 MiB of HBM per device.

v0:
```python
import jax
import jax.numpy as jnp
from jax import lax
from jax.sharding import PartitionSpec as P

INNER = 3
learn_rate = 0.02
inner_beta = 0.9
slow_beta = 0.5


def passed_along(block, axis, distance):
    devices = range(lax.axis_size(axis))
    route = [((i - distance) % len(devices), i) for i in devices]
    return lax.ppermute(block, axis, route)


def gelu_pair(pre):
    coeff = 0.7978845608028654
    inner = coeff * (pre + 0.044715 * pre * pre * pre)
    tanh_val = jnp.tanh(inner)
    value = 0.5 * pre * (1.0 + tanh_val)
    slope = 0.5 * (1.0 + tanh_val) + 0.5 * pre * (1.0 - tanh_val * tanh_val) * coeff * (
        1.0 + 3.0 * 0.044715 * pre * pre
    )
    return (value, slope)


def body(tokens, targets, row_ids, anchor, momentum, slow):
    row_count = tokens.shape[0]
    scale = 1.0 / row_count
    weights = anchor
    moment = momentum[0]
    for step in range(INNER):
        if step > 0:
            incoming = passed_along(weights.astype(jnp.bfloat16), "replica", 2 ** (step - 1))
            weights = 0.5 * (weights + incoming.astype(jnp.float32))
        picks = row_ids[0, step]
        inputs = jnp.take(tokens, picks, axis=0)
        wanted = jnp.take(targets, picks, axis=0)
        weights_bf = weights.astype(jnp.bfloat16)
        pre = jnp.dot(inputs, weights_bf[0], preferred_element_type=jnp.float32)
        value, slope = gelu_pair(pre)
        hidden = value.astype(jnp.bfloat16)
        partial_out = lax.dot_general(
            hidden, weights_bf[1], (((1,), (1,)), ((), ())), preferred_element_type=jnp.float32
        )
        summed = lax.psum(partial_out, "tensor")
        error = ((summed - wanted.astype(jnp.float32)) * scale).astype(jnp.bfloat16)
        back = (jnp.dot(error, weights_bf[1], preferred_element_type=jnp.float32) * slope).astype(
            jnp.bfloat16
        )
        grad_in = lax.dot_general(
            inputs, back, (((0,), (0,)), ((), ())), preferred_element_type=jnp.float32
        )
        grad_out = lax.dot_general(
            error, hidden, (((0,), (0,)), ((), ())), preferred_element_type=jnp.float32
        )
        moment = inner_beta * moment + jnp.stack([grad_in, grad_out])
        weights = weights - learn_rate * moment
    replicas = lax.axis_size("replica")
    total = lax.psum(weights, "replica")
    mean = total / replicas
    slow_new = slow_beta * slow + (anchor - mean) / learn_rate
    anchor_new = anchor - learn_rate * slow_new
    return (anchor_new, slow_new, moment[None])


def solution(mesh):
    return jax.shard_map(
        body,
        mesh=mesh,
        in_specs=(
            P("replica", None),
            P("replica", None),
            P("replica", None, None),
            P(None, None, "tensor"),
            P("replica", None, None, "tensor"),
            P(None, None, "tensor"),
        ),
        out_specs=(
            P(None, None, "tensor"),
            P(None, None, "tensor"),
            P("replica", None, None, "tensor"),
        ),
        check_vma=False,
    )
```

profile of v0, /device:TPU:0, one launch (start us, length us, event | category | flops | bytes accessed | tf_op | source)
XLA Modules:
  0.0 625.0 jit_solution(4985330071211238763)
XLA Ops:
  7.2 0.8 fusion.103
  8.0 3.8 convert_element_type.57
  11.8 2.0 gather_fusion
  13.9 2.1 fusion.34
  16.0 1.0 copy-done.19
  17.0 2.1 fusion.56
  19.2 1.1 copy-done.2
  20.4 2.8 gather_fusion.1
  23.1 105.8 %all-reduce.5.cloned.1.call-done = f32[512,1024]{1,0:T(8,128)} async-done(((f32[512,1024]{1,0:T(8,128)}), f32[512,1024]{1,0:T(8,128)}) %all-reduce.5.cloned.1.call-update) | async-done | bytes 2097168 | tf_op jit(solution)/shard_map/psum | solution.py:48
  128.9 5.6 fusion.13
  134.5 3.5 fusion.99
  138.0 1.8 copy-done.11
  139.8 0.8 copy-done.12
  140.6 4.5 fusion.83
  145.1 2.1 gather_fusion.2
  147.2 25.8 %collective-permute-done = bf16[2,1024,512]{2,1,0:T(8,128)(2,1)} collective-permute-done((bf16[2,1024,512]{2,1,0:T(8,128)(2,1)}, bf16[2,1024,512]{2,1,0:T(8,128)(2,1)}, u32[]{:S(2)}, u32[]{:S(2)}) %collective-permute-start) | collective-permute-done | bytes 2097184 | tf_op jit(solution)/shard_map/ppermute | solution.py:15
  173.0 5.3 fusion.6
  178.3 0.8 fusion.33
  179.1 0.6 copy-done.16
  179.7 1.0 copy-done.20
  180.6 2.1 fusion.57
  182.8 0.2 all-reduce.9.cloned.1.call-start
  183.0 2.8 gather_fusion.3
  185.8 100.5 %all-reduce.7.cloned.1.call-done = f32[512,1024]{1,0:T(8,128)} async-done(((f32[512,1024]{1,0:T(8,128)}), f32[512,1024]{1,0:T(8,128)}) %all-reduce.7.cloned.1.call-update) | async-done | bytes 2097168 | tf_op jit(solution)/shard_map/psum | solution.py:48
  286.3 5.6 fusion.12
  291.9 3.5 fusion.100
  295.4 1.8 copy-done.5
  297.2 0.8 copy-done.8
  298.0 5.1 fusion.102
  303.1 1.6 collective-permute-start.1
  304.6 2.1 gather_fusion.4
  306.7 45.4 %collective-permute-done.1 = bf16[2,1024,512]{2,1,0:T(8,128)(2,1)} collective-permute-done((bf16[2,1024,512]{2,1,0:T(8,128)(2,1)}, bf16[2,1024,512]{2,1,0:T(8,128)(2,1)}, u32[]{:S(2)}, u32[]{:S(2)}) %collective-permute-start.1) | collective-permute-done | bytes 2097184 | tf_op jit(solution)/shard_map/ppermute | solution.py:15
  352.1 3.6 fusion.7
  355.7 0.8 fusion.32
  356.5 0.6 copy-done.17
  357.0 2.2 fusion.58
  359.3 0.3 all-reduce.11.cloned.1.call-start
  359.5 2.1 gather_fusion.5
  361.6 101.4 %all-reduce.9.cloned.1.call-done = f32[512,1024]{1,0:T(8,128)} async-done(((f32[512,1024]{1,0:T(8,128)}), f32[512,1024]{1,0:T(8,128)}) %all-reduce.9.cloned.1.call-update) | async-done | bytes 2097168 | tf_op jit(solution)/shard_map/psum | solution.py:48
  463.0 5.4 fusion.11
  468.4 3.4 fusion.101
  471.9 1.3 copy-done.14
  473.2 0.5 copy-done.7
  473.7 0.8 copy-done.9
  474.5 5.4 fusion.1
  479.9 7.7 %fusion.5 = f32[1,2,1024,512]{3,2,1,0:T(8,128)} fusion(f32[1,1,1024,512]{3,2,1,0:T(8,128)} %bitcast.51, f32[1,1,1024,512]{3,2,1,0:T(8,128)} %bitcast.48, f32[1,1,1024,512]{3,2,1,0:T(8,128)} %bitcast.47, f32[1,1,1024,512]{3,2,1,0:T(8,128)S(1)} %bitcast.44, f32[1,1,1024,512]{3,2,1,0:T(8,128)} %bitcast.55, f32[1,1,1024,512]{3,2,1,0:T(8,128)} %bitcast.53, ...), kind=kLoop, calls=%fused_computation.15 | loop fusion | flops 9437184 | bytes 20971520 | tf_op jit(solution)/shard_map/add | solution.py:59
  487.6 120.6 %all-reduce.11.cloned.1.call-done = f32[2,1024,512]{2,1,0:T(8,128)} async-done(((f32[2,1024,512]{2,1,0:T(8,128)}), f32[2,1024,512]{2,1,0:T(8,128)}) %all-reduce.11.cloned.1.call-update) | async-done | bytes 4194320 | tf_op jit(solution)/shard_map/psum | solution.py:62
  608.2 10.2 %multiply_subtract_fusion = (f32[2,1024,512]{2,1,0:T(8,128)}, f32[2,1024,512]{2,1,0:T(8,128)}) fusion(f32[2,1024,512]{2,1,0:T(8,128)} %param.11, f32[2,1024,512]{2,1,0:T(8,128)} %all-reduce.11.cloned.1.call-done, f32[2,1024,512]{2,1,0:T(8,128)} %param.13), kind=kLoop, calls=%fused_computation.16 | loop fusion | flops 7340032 | bytes 20971520 | tf_op jit(solution)/shard_map/sub | solution.py:65
  (48 shorter events, 0.3 us)
Async XLA Ops:
  7.2 4.7 copy-start
  7.2 121.7 %all-reduce.5.cloned.1.call-start = ((), (), s32[]{:S(2)}) async-start(), calls=%async_computation | async-start | bytes 4194304 | tf_op jit(solution)/shard_map/psum | solution.py:48
  13.9 3.1 copy-start.15
  16.0 1.0 copy-start.19
  19.1 1.2 copy-start.2
  19.2 267.1 %all-reduce.7.cloned.1.call-start = ((), (), s32[]{:S(2)}) async-start(), calls=%async_computation.1 | async-start | bytes 4194304 | tf_op jit(solution)/shard_map/psum | solution.py:48
  134.5 3.5 copy-start.3
  134.5 5.3 copy-start.11
  134.5 6.1 copy-start.12
  138.0 7.1 %copy-start.13 = (f32[1024,512]{1,0:T(8,128)}, f32[1024,512]{1,0:T(8,128)S(1)}, u32[]{:S(2)}) copy-start(f32[1024,512]{1,0:T(8,128)S(1)} %fusion.99) | copy-start | bytes 6291460
  145.1 27.9 %collective-permute-start = (bf16[2,1024,512]{2,1,0:T(8,128)(2,1)}, bf16[2,1024,512]{2,1,0:T(8,128)(2,1)}, u32[]{:S(2)}, u32[]{:S(2)}) collective-permute-start(bf16[2,1024,512]{2,1,0:T(8,128)(2,1)} %get-tuple-element.8), channel_id=1, source_target_pairs={{120,0},{0,8},{8,16},{16,24},{24,32},{32,40},{40,48},{48,56},{56,6... | collective-permute-start | bytes 6291464 | tf_op jit(solution)/shard_map/ppermute | solution.py:15
  178.3 1.4 copy-start.16
  179.7 1.0 copy-start.20
  182.8 280.2 %all-reduce.9.cloned.1.call-start = ((), (), s32[]{:S(2)}) async-start(), calls=%async_computation.2 | async-start | bytes 4194304 | tf_op jit(solution)/shard_map/psum | solution.py:48
  291.9 3.5 copy-start.4
  291.9 5.3 copy-start.5
  291.9 6.1 copy-start.8
  295.4 7.7 %copy-start.10 = (f32[1024,512]{1,0:T(8,128)}, f32[1024,512]{1,0:T(8,128)S(1)}, u32[]{:S(2)}) copy-start(f32[1024,512]{1,0:T(8,128)S(1)} %fusion.100) | copy-start | bytes 6291460
  303.1 49.0 %collective-permute-start.1 = (bf16[2,1024,512]{2,1,0:T(8,128)(2,1)}, bf16[2,1024,512]{2,1,0:T(8,128)(2,1)}, u32[]{:S(2)}, u32[]{:S(2)}) collective-permute-start(bf16[2,1024,512]{2,1,0:T(8,128)(2,1)} %get-tuple-element.6), channel_id=1, source_target_pairs={{112,0},{120,8},{0,16},{8,24},{16,32},{24,40},{32,48},{40,56},{48,... | collective-permute-start | bytes 6291464 | tf_op jit(solution)/shard_map/ppermute | solution.py:15
  355.7 1.3 copy-start.17
  357.0 2.2 copy-start.21
  359.3 249.0 %all-reduce.11.cloned.1.call-start = ((), (), s32[]{:S(2)}) async-start(), calls=%async_computation.3 | async-start | bytes 8388608 | tf_op jit(solution)/shard_map/psum | solution.py:62
  361.6 101.4 %copy-start.18 = (bf16[512,1024]{1,0:T(8,128)(2,1)}, bf16[512,1024]{1,0:T(8,128)(2,1)S(1)}, u32[]{:S(2)}) copy-start(bf16[512,1024]{1,0:T(8,128)(2,1)S(1)} %gather_fusion.5) | copy-start | bytes 3145732
  468.4 4.8 copy-start.6
  468.4 5.3 copy-start.7
  468.4 6.1 copy-start.9
  471.9 1.3 copy-start.14
  608.2 10.2 %copy-start.1 = (bf16[512,1024]{1,0:T(8,128)(2,1)S(1)}, bf16[512,1024]{1,0:T(8,128)(2,1)}, u32[]{:S(2)}) copy-start(bf16[512,1024]{1,0:T(8,128)(2,1)} %param.8) | copy-start | bytes 3145732
Sparse Core Ops, SparseCore 0:
  19.3 109.5 all-reduce.4
  182.9 103.3 all-reduce.6
  359.4 103.5 all-reduce.8
  480.1 128.1 all-reduce.10
where the time goes:
time: 625 us
  waiting for transfers between devices  500 us (80%)
  other arithmetic  45.6 us (7%)
  matrix products  37 us (6%)
  local copies, waits for them, and re-layouts  26.7 us (4%)
  between operations  14 us (2%)
    psum x3, waiting for transfers between devices, body(): summed = lax.psum(partial_out, 'tensor')  308 us
    psum x1, waiting for transfers between devices, body(): total = lax.psum(weights, 'replica')  121 us
    ppermute x2, waiting for transfers between devices, passed_along(): return lax.ppermute(block, axis, route)  71.2 us
    dot_general x3, matrix products, body(): lax.dot_general(inputs, back, (((0,), (0,)), ((), ())), preferred_element...  16.6 us
    convert_element_type x3, other arithmetic, body(): weights_bf = weights.astype(jnp.bfloat16)  12.7 us
  transfers between devices with their start and end apart: 6, of which 6 were waited for; matrix products, arithmetic and copies ran while one was open for 3% of the time, Pallas kernels for 0%

commit v1 on v0

--- a/solution.py
+++ b/solution.py
@@ -59,7 +59,7 @@
         moment = inner_beta * moment + jnp.stack([grad_in, grad_out])
         weights = weights - learn_rate * moment
     replicas = lax.axis_size("replica")
-    total = lax.psum(weights, "replica")
+    total = lax.all_gather(weights, "replica").sum(axis=0)
     mean = total / replicas
     slow_new = slow_beta * slow + (anchor - mean) / learn_rate
     anchor_new = anchor - learn_rate * slow_new

time: 625 us -> 849 us (1.36)
  waiting for transfers between devices: 500 us -> 698 us
  other arithmetic: 45.6 us -> 68.8 us
    all_gather x0 -> x1, waiting for transfers between devices: none -> 320 us  [body(): total = lax.all_gather(weights, 'replica').sum(axis=0)]
    psum x1 -> x0, waiting for transfers between devices: 121 us -> none  [body(): total = lax.psum(weights, 'replica')]
    reduce_sum x0 -> x1, other arithmetic: none -> 23.2 us  [body(): total = lax.all_gather(weights, 'replica').sum(axis=0)]
  transfers between devices with their start and end apart: 6 -> 6, of which waited for: 6 -> 6; matrix products, arithmetic and copies ran while one was open for 3% -> 2% of each run, Pallas kernels for 0% -> 0%
where the time goes in v1:
time: 849 us; the launch traced here: 847 us
  waiting for transfers between devices  698 us (82%)
  other arithmetic  68.8 us (8%)
  matrix products  37 us (4%)
  local copies, waits for them, and re-layouts  26.9 us (3%)
  between operations  14 us (2%)
    all_gather x1, waiting for transfers between devices, body(): total = lax.all_gather(weights, 'replica').sum(axis=0)  320 us
    psum x3, waiting for transfers between devices, body(): summed = lax.psum(partial_out, 'tensor')  308 us
    ppermute x2, waiting for transfers between devices, passed_along(): return lax.ppermute(block, axis, route)  71.1 us
    reduce_sum x1, other arithmetic, body(): total = lax.all_gather(weights, 'replica').sum(axis=0)  23.2 us
  transfers between devices with their start and end apart: 6, of which 6 were waited for; matrix products, arithmetic and copies ran while one was open for 2% of the time, Pallas kernels for 0%

profile of v1, /device:TPU:0, one launch (start us, length us, event | category | flops | bytes accessed | tf_op | source)
XLA Modules:
  0.0 847.2 jit_solution(18049190229910486934)
XLA Ops:
  7.2 0.8 fusion.103
  8.1 3.8 convert_element_type.57
  11.8 2.0 gather_fusion
  13.9 2.1 fusion.34
  16.0 1.0 copy-done.19
  17.0 2.1 fusion.56
  19.2 1.1 copy-done.2
  20.4 2.8 gather_fusion.1
  23.1 105.8 %all-reduce.4.cloned.1.call-done = f32[512,1024]{1,0:T(8,128)} async-done(((f32[512,1024]{1,0:T(8,128)}), f32[512,1024]{1,0:T(8,128)}) %all-reduce.4.cloned.1.call-update) | async-done | bytes 2097168 | tf_op jit(solution)/shard_map/psum | solution.py:48
  128.9 5.6 fusion.13
  134.5 3.5 fusion.99
  138.0 1.8 copy-done.11
  139.8 0.8 copy-done.12
  140.6 4.5 fusion.83
  145.1 2.1 gather_fusion.2
  147.1 25.8 %collective-permute-done = bf16[2,1024,512]{2,1,0:T(8,128)(2,1)} collective-permute-done((bf16[2,1024,512]{2,1,0:T(8,128)(2,1)}, bf16[2,1024,512]{2,1,0:T(8,128)(2,1)}, u32[]{:S(2)}, u32[]{:S(2)}) %collective-permute-start) | collective-permute-done | bytes 2097184 | tf_op jit(solution)/shard_map/ppermute | solution.py:15
  172.9 5.3 fusion.6
  178.3 0.8 fusion.33
  179.0 0.6 copy-done.16
  179.7 1.1 copy-done.20
  180.7 2.1 fusion.57
  183.1 2.8 gather_fusion.3
  185.9 100.6 %all-reduce.6.cloned.1.call-done = f32[512,1024]{1,0:T(8,128)} async-done(((f32[512,1024]{1,0:T(8,128)}), f32[512,1024]{1,0:T(8,128)}) %all-reduce.6.cloned.1.call-update) | async-done | bytes 2097168 | tf_op jit(solution)/shard_map/psum | solution.py:48
  286.4 5.6 fusion.12
  292.1 3.5 fusion.100
  295.6 1.8 copy-done.5
  297.4 0.8 copy-done.8
  298.2 5.1 fusion.102
  303.3 1.6 collective-permute-start.1
  304.8 2.1 gather_fusion.4
  306.9 45.4 %collective-permute-done.1 = bf16[2,1024,512]{2,1,0:T(8,128)(2,1)} collective-permute-done((bf16[2,1024,512]{2,1,0:T(8,128)(2,1)}, bf16[2,1024,512]{2,1,0:T(8,128)(2,1)}, u32[]{:S(2)}, u32[]{:S(2)}) %collective-permute-start.1) | collective-permute-done | bytes 2097184 | tf_op jit(solution)/shard_map/ppermute | solution.py:15
  352.3 3.6 fusion.7
  355.9 0.8 fusion.32
  356.6 0.6 copy-done.17
  357.2 2.2 fusion.58
  359.4 0.3 all-gather.3.cloned.1.call-start
  359.7 2.1 gather_fusion.5
  361.8 101.4 %all-reduce.8.cloned.1.call-done = f32[512,1024]{1,0:T(8,128)} async-done(((f32[512,1024]{1,0:T(8,128)}), f32[512,1024]{1,0:T(8,128)}) %all-reduce.8.cloned.1.call-update) | async-done | bytes 2097168 | tf_op jit(solution)/shard_map/psum | solution.py:48
  463.2 5.3 fusion.11
  468.5 3.4 fusion.101
  472.0 1.3 copy-done.14
  473.3 0.5 copy-done.7
  473.8 0.8 copy-done.9
  474.6 5.4 fusion.1
  480.1 7.7 fusion.5
  487.7 319.5 %all-gather.3.cloned.1.call-done = f32[32,1024,512]{2,1,0:T(8,128)} async-done(((f32[2,1024,512]{2,1,0:T(8,128)}), f32[32,1024,512]{2,1,0:T(8,128)}) %all-gather.3.cloned.1.call-update) | async-done | bytes 67108880 | tf_op jit(solution)/shard_map/all_gather | solution.py:62
  807.3 23.2 %reduce_sum.9 = f32[2,1024,512]{2,1,0:T(8,128)} reduce(f32[16,2,1024,512]{3,2,1,0:T(8,128)} %bitcast.16, f32[]{:T(128)} %constant.14.clone.1), dimensions={0}, to_apply=%region_3.5 | reduce | flops 15728640 | bytes 71303168 | tf_op jit(solution)/shard_map/reduce_sum | solution.py:62
  830.4 10.2 %multiply_subtract_fusion = (f32[2,1024,512]{2,1,0:T(8,128)}, f32[2,1024,512]{2,1,0:T(8,128)}) fusion(f32[2,1024,512]{2,1,0:T(8,128)} %param.11, f32[2,1024,512]{2,1,0:T(8,128)} %reduce_sum.9, f32[2,1024,512]{2,1,0:T(8,128)} %param.13), kind=kLoop, calls=%fused_computation.16 | loop fusion | flops 7340032 | bytes 20971520 | tf_op jit(solution)/shard_map/sub | solution.py:65
  (49 shorter events, 0.5 us)
Async XLA Ops:
  7.2 4.7 copy-start
  7.2 121.7 %all-reduce.4.cloned.1.call-start = ((), (), s32[]{:S(2)}) async-start(), calls=%async_computation | async-start | bytes 4194304 | tf_op jit(solution)/shard_map/psum | solution.py:48
  13.9 3.1 copy-start.15
  16.0 1.0 copy-start.19
  19.1 1.2 copy-start.2
  19.2 267.3 %all-reduce.6.cloned.1.call-start = ((), (), s32[]{:S(2)}) async-start(), calls=%async_computation.1 | async-start | bytes 4194304 | tf_op jit(solution)/shard_map/psum | solution.py:48
  134.5 3.5 copy-start.3
  134.5 5.3 copy-start.11
  134.5 6.1 copy-start.12
  138.0 7.1 copy-start.13
  145.0 27.9 %collective-permute-start = (bf16[2,1024,512]{2,1,0:T(8,128)(2,1)}, bf16[2,1024,512]{2,1,0:T(8,128)(2,1)}, u32[]{:S(2)}, u32[]{:S(2)}) collective-permute-start(bf16[2,1024,512]{2,1,0:T(8,128)(2,1)} %get-tuple-element.8), channel_id=1, source_target_pairs={{120,0},{0,8},{8,16},{16,24},{24,32},{32,40},{40,48},{48,56},{56,6... | collective-permute-start | bytes 6291464 | tf_op jit(solution)/shard_map/ppermute | solution.py:15
  178.3 1.4 copy-start.16
  179.7 1.1 copy-start.20
  182.9 280.3 %all-reduce.8.cloned.1.call-start = ((), (), s32[]{:S(2)}) async-start(), calls=%async_computation.2 | async-start | bytes 4194304 | tf_op jit(solution)/shard_map/psum | solution.py:48
  292.1 3.5 copy-start.4
  292.1 5.3 copy-start.5
  292.1 6.1 copy-start.8
  295.6 7.7 copy-start.10
  303.3 49.0 %collective-permute-start.1 = (bf16[2,1024,512]{2,1,0:T(8,128)(2,1)}, bf16[2,1024,512]{2,1,0:T(8,128)(2,1)}, u32[]{:S(2)}, u32[]{:S(2)}) collective-permute-start(bf16[2,1024,512]{2,1,0:T(8,128)(2,1)} %get-tuple-element.6), channel_id=1, source_target_pairs={{112,0},{120,8},{0,16},{8,24},{16,32},{24,40},{32,48},{40,56},{48,... | collective-permute-start | bytes 6291464 | tf_op jit(solution)/shard_map/ppermute | solution.py:15
  355.8 1.4 copy-start.17
  357.2 2.2 copy-start.21
  359.4 447.9 %all-gather.3.cloned.1.call-start = ((), (), s32[]{:S(2)}) async-start(), calls=%async_computation.3 | async-start | bytes 71303168 | tf_op jit(solution)/shard_map/all_gather | solution.py:62
  361.8 101.4 %copy-start.18 = (bf16[512,1024]{1,0:T(8,128)(2,1)}, bf16[512,1024]{1,0:T(8,128)(2,1)S(1)}, u32[]{:S(2)}) copy-start(bf16[512,1024]{1,0:T(8,128)(2,1)S(1)} %gather_fusion.5) | copy-start | bytes 3145732
  468.5 4.8 copy-start.6
  468.5 5.3 copy-start.7
  468.5 6.1 copy-start.9
  472.0 1.4 copy-start.14
  830.4 10.2 %copy-start.1 = (bf16[512,1024]{1,0:T(8,128)(2,1)S(1)}, bf16[512,1024]{1,0:T(8,128)(2,1)}, u32[]{:S(2)}) copy-start(bf16[512,1024]{1,0:T(8,128)(2,1)} %param.8) | copy-start | bytes 3145732
Sparse Core Ops, SparseCore 0:
  19.3 109.5 all-reduce.3
  183.0 103.4 all-reduce.5
  359.5 103.6 all-reduce.7
  480.2 327.0 all-gather.2
